TPU v7x, 32 devices: a whole 2x2x4 slice. The times are simulated.
32 devices in a mesh: dp: 8 (over z, x), row: 2 (over y), col: 2 (over core).
Axes of the slice: x: 2, y: 2, z: 4, core: 2. Of those that a mesh axis runs over, the one named last changes fastest.
Arguments:
- block_in: float32 [8192, 768], P(('dp', 'row'), 'col'), may hold values from -6 to 6
- upstream: float32 [8192, 768], P(('dp', 'row'), 'col'), may hold values from -6 to 6
- norm_params: float32 [4, 768], P(None, 'col'), may hold values from -0.5 to 1.5
- w_qkv: float32 [3, 12, 64, 768], P(None, 'row', 'dp', 'col'), may hold values from -1.4433757 to 1.4433757
- w_attn: float32 [12, 64, 768], P('row', 'dp', 'col'), may hold values from -0.875 to 0.875
- w_up: float32 [3072, 768], P(('dp', 'row'), 'col'), may hold values from -0.21875 to 0.21875
- w_down: float32 [3072, 768], P(('dp', 'row'), 'col'), may hold values from -0.109375 to 0.109375
- mom_norm: float32 [2, 4, 768], P(None, None, 'col'), may hold values from -0.224 to 0.224, as said below
- mom_qkv: float32 [2, 3, 12, 64, 768], P(None, None, 'row', 'dp', 'col'), may hold values from -0.16 to 0.16, as said below
- mom_attn: float32 [2, 12, 64, 768], P(None, 'row', 'dp', 'col'), may hold values from -0.048 to 0.048, as said below
- mom_up: float32 [2, 3072, 768], P(None, ('dp', 'row'), 'col'), may hold values from -0.128 to 0.128, as said below
- mom_down: float32 [2, 3072, 768], P(None, ('dp', 'row'), 'col'), may hold values from -0.208 to 0.208, as said below
Outputs:
- block_out: float32 [8192, 768], P(('dp', 'row'), 'col')
- input_grad: float32 [8192, 768], P(('dp', 'row'), 'col')
- grad_norm: float32 [4, 768], P(None, 'col')
- grad_qkv: float32 [3, 12, 64, 768], P(None, 'row', 'dp', 'col')
- grad_attn: float32 [12, 64, 768], P('row', 'dp', 'col')
- grad_up: float32 [3072, 768], P(('dp', 'row'), 'col')
- grad_down: float32 [3072, 768], P(('dp', 'row'), 'col')
- new_norm: float32 [4, 768], P(None, 'col')
- new_qkv: float32 [3, 12, 64, 768], P(None, 'row', 'dp', 'col')
- new_attn: float32 [12, 64, 768], P('row', 'dp', 'col')
- new_up: float32 [3072, 768], P(('dp', 'row'), 'col')
- new_down: float32 [3072, 768], P(('dp', 'row'), 'col')
- new_mom_norm: float32 [2, 4, 768], P(None, None, 'col')
- new_mom_qkv: float32 [2, 3, 12, 64, 768], P(None, None, 'row', 'dp', 'col')
- new_mom_attn: float32 [2, 12, 64, 768], P(None, 'row', 'dp', 'col')
- new_mom_up: float32 [2, 3072, 768], P(None, ('dp', 'row'), 'col')
- new_mom_down: float32 [2, 3072, 768], P(None, ('dp', 'row'), 'col')
Inputs may be any that keep to these rules, and one draw needn't show every extreme that they name: `mom_norm`: second moments are positive. `mom_qkv`: second moments are positive. `mom_attn`: second moments are positive. `mom_up`: second moments are positive. `mom_down`: second moments are positive.
All inputs are finite; a program needn't handle non-finite values.
Results may differ from a plain program's by a relative error of at most 0.012.
The roundings to bfloat16 on the way count: a program that leaves them out, or rounds other values in their place, can miss the bound.
Values may be sent and summed in bfloat16 or wider, within the bound.
A program may use at most 128 MiB of HBM per device.

v0:
```python
import math
import jax
import jax.numpy as jnp
from jax import lax
from jax.sharding import PartitionSpec as P

SEQ = 512
STEP = 4
norm_eps = 1e-05
adam_eps = 1e-08
beta_one = 0.9
beta_two = 0.95
learn_rate = 0.02
decay_rate = 0.1
gelu_coef = math.sqrt(2.0 / math.pi)
cubic_coef = 0.044715
masked_score = -1e30


def smooth_pair(values):
    squared = values * values
    bent = jnp.tanh(gelu_coef * (values + cubic_coef * squared * values))
    smooth = 0.5 * values * (1.0 + bent)
    slope = 0.5 * (1.0 + bent) + 0.5 * values * (1.0 - bent * bent) * gelu_coef * (
        1.0 + 3.0 * cubic_coef * squared
    )
    return (smooth, slope)


def feature_total(pieces):
    return lax.psum(pieces, "col")


def normalize(rows_in, gain_row, shift_row):
    feature_count = rows_in.shape[1] * lax.axis_size("col")
    (row_total,) = feature_total((jnp.sum(rows_in, axis=1, keepdims=True),))
    center = rows_in - row_total / feature_count
    (square_total,) = feature_total((jnp.sum(center * center, axis=1, keepdims=True),))
    spread = square_total / feature_count
    inverse = lax.rsqrt(spread + norm_eps)
    normal = center * inverse
    return (normal, inverse, (normal * gain_row + shift_row).astype(jnp.bfloat16))


def norm_back(grad_normed, normal, inverse, gain_row):
    feature_count = grad_normed.shape[1] * lax.axis_size("col")
    scaled = grad_normed * gain_row
    first_total, second_total = feature_total(
        (jnp.sum(scaled, axis=1, keepdims=True), jnp.sum(scaled * normal, axis=1, keepdims=True))
    )
    return inverse * (
        scaled - first_total / feature_count - normal * (second_total / feature_count)
    )


def rows_then_cols(local_rows, weight):
    everyone = lax.all_gather(local_rows, "row", axis=0, tiled=True)
    return (
        lax.psum_scatter(
            lax.dot_general(
                everyone, weight, (((1,), (1,)), ((), ())), preferred_element_type=jnp.float32
            ),
            "col",
            scatter_dimension=0,
            tiled=True,
        ),
        everyone,
    )


def cols_then_rows(local_rows, weight):
    everyone = lax.all_gather(local_rows, "col", axis=0, tiled=True)
    return (
        lax.psum_scatter(
            jnp.dot(everyone, weight, preferred_element_type=jnp.float32),
            "row",
            scatter_dimension=0,
            tiled=True,
        ),
        everyone,
    )


def token_product(left_rows, right_rows):
    return lax.dot_general(
        left_rows, right_rows, (((0,), (0,)), ((), ())), preferred_element_type=jnp.float32
    )


def causal_mask(length):
    return lax.broadcasted_iota(jnp.int32, (length, length), 0) >= lax.broadcasted_iota(
        jnp.int32, (length, length), 1
    )


def seq_scores(qkv_seq):
    score_scale = 1.0 / math.sqrt(qkv_seq.shape[3])
    scores = (
        jnp.einsum("qhd,khd->hqk", qkv_seq[:, 0], qkv_seq[:, 1], preferred_element_type=jnp.float32)
        * score_scale
    )
    return (jnp.where(causal_mask(qkv_seq.shape[0])[None], scores, masked_score), score_scale)


def attend(qkv_seq):
    scores, score_scale = seq_scores(qkv_seq)
    highest = jnp.max(scores, axis=2, keepdims=True)
    log_total = highest + jnp.log(jnp.sum(jnp.exp(scores - highest), axis=2, keepdims=True))
    attn_probs = jnp.exp(scores - log_total).astype(jnp.bfloat16)
    mixed = jnp.einsum(
        "hqk,khd->qhd", attn_probs, qkv_seq[:, 2], preferred_element_type=jnp.float32
    )
    return (mixed.astype(jnp.bfloat16).reshape(qkv_seq.shape[0], -1), log_total)


def attend_back(operands):
    qkv_seq, grad_mixed, log_total = operands
    grad_mixed = grad_mixed.reshape(qkv_seq.shape[0], qkv_seq.shape[2], qkv_seq.shape[3])
    scores, score_scale = seq_scores(qkv_seq)
    attn_probs = jnp.exp(scores - log_total)
    grad_values = jnp.einsum(
        "hqk,qhd->khd",
        attn_probs.astype(jnp.bfloat16),
        grad_mixed,
        preferred_element_type=jnp.float32,
    )
    grad_probs = jnp.einsum(
        "qhd,khd->hqk", grad_mixed, qkv_seq[:, 2], preferred_element_type=jnp.float32
    )
    delta_rows = jnp.sum(attn_probs * grad_probs, axis=2, keepdims=True)
    grad_scores = (attn_probs * (grad_probs - delta_rows) * score_scale).astype(jnp.bfloat16)
    grad_queries = jnp.einsum(
        "hqk,khd->qhd", grad_scores, qkv_seq[:, 1], preferred_element_type=jnp.float32
    )
    grad_keys = jnp.einsum(
        "hqk,qhd->khd", grad_scores, qkv_seq[:, 0], preferred_element_type=jnp.float32
    )
    return jnp.stack([grad_queries, grad_keys, grad_values], axis=1).astype(jnp.bfloat16)


def adam_step(weight, grad, moments, decay):
    first_moment = beta_one * moments[0] + (1.0 - beta_one) * grad
    second_moment = beta_two * moments[1] + (1.0 - beta_two) * grad * grad
    step_size = (
        first_moment
        / (1.0 - beta_one**STEP)
        / (jnp.sqrt(second_moment / (1.0 - beta_two**STEP)) + adam_eps)
    )
    return (
        weight - learn_rate * (step_size + decay * weight),
        jnp.stack([first_moment, second_moment]),
    )


def on_device(
    block_in,
    upstream,
    norm_params,
    w_qkv,
    w_attn,
    w_up,
    w_down,
    mom_norm,
    mom_qkv,
    mom_attn,
    mom_up,
    mom_down,
):
    qkv_block, attn_block, up_block, down_block = (
        lax.all_gather(w_qkv.astype(jnp.bfloat16), "dp", axis=2, tiled=True),
        lax.all_gather(w_attn.astype(jnp.bfloat16), "dp", axis=1, tiled=True),
        lax.all_gather(w_up.astype(jnp.bfloat16), "dp", axis=0, tiled=True),
        lax.all_gather(w_down.astype(jnp.bfloat16), "dp", axis=0, tiled=True),
    )
    heads_here = qkv_block.shape[1]
    head_size = qkv_block.shape[2]
    feature_here = qkv_block.shape[3]
    qkv_mat = qkv_block.reshape(3 * heads_here * head_size, feature_here)
    attn_mat = attn_block.reshape(heads_here * head_size, feature_here)
    normal_one, inverse_one, normed_one = normalize(block_in, norm_params[0], norm_params[1])
    triples, normed_one_all = rows_then_cols(normed_one, qkv_mat)
    triples = triples.astype(jnp.bfloat16).reshape(-1, SEQ, 3, heads_here, head_size)
    mixed, log_total = lax.map(attend, triples)
    mixed = mixed.reshape(-1, heads_here * head_size)
    attn_branch, mixed_all = cols_then_rows(mixed, attn_mat)
    middle = block_in + attn_branch
    normal_two, inverse_two, normed_two = normalize(middle, norm_params[2], norm_params[3])
    hidden_pre, normed_two_all = rows_then_cols(normed_two, up_block)
    activated, slope = smooth_pair(hidden_pre)
    activated = activated.astype(jnp.bfloat16)
    mlp_branch, activated_all = cols_then_rows(activated, down_block)
    block_out = middle + mlp_branch
    upstream_b = upstream.astype(jnp.bfloat16)
    grad_hidden, upstream_all = rows_then_cols(upstream_b, down_block)
    grad_down = token_product(activated_all, upstream_all)
    grad_pre = (grad_hidden * slope).astype(jnp.bfloat16)
    grad_normed_two, grad_pre_all = cols_then_rows(grad_pre, up_block)
    grad_up = token_product(grad_pre_all, normed_two_all)
    middle_grad = upstream + norm_back(grad_normed_two, normal_two, inverse_two, norm_params[2])
    middle_b = middle_grad.astype(jnp.bfloat16)
    grad_mixed, middle_all = rows_then_cols(middle_b, attn_mat)
    grad_attn = token_product(mixed_all, middle_all).reshape(heads_here, head_size, feature_here)
    grad_mixed = grad_mixed.astype(jnp.bfloat16).reshape(
        triples.shape[0], SEQ, heads_here * head_size
    )
    grad_triples = lax.map(attend_back, (triples, grad_mixed, log_total))
    grad_triples = grad_triples.reshape(-1, 3 * heads_here * head_size)
    grad_normed_one, triples_all = cols_then_rows(grad_triples, qkv_mat)
    grad_qkv = token_product(triples_all, normed_one_all).reshape(
        3, heads_here, head_size, feature_here
    )
    input_grad = middle_grad + norm_back(grad_normed_one, normal_one, inverse_one, norm_params[0])
    norm_terms = jnp.stack(
        [
            jnp.sum(grad_normed_one * normal_one, axis=0),
            jnp.sum(grad_normed_one, axis=0),
            jnp.sum(grad_normed_two * normal_two, axis=0),
            jnp.sum(grad_normed_two, axis=0),
        ]
    )
    (grad_norm,) = lax.psum((norm_terms,), ("dp", "row"))
    grad_qkv, grad_attn, grad_up, grad_down = (
        lax.psum_scatter(grad_qkv, "dp", scatter_dimension=2, tiled=True),
        lax.psum_scatter(grad_attn, "dp", scatter_dimension=1, tiled=True),
        lax.psum_scatter(grad_up, "dp", scatter_dimension=0, tiled=True),
        lax.psum_scatter(grad_down, "dp", scatter_dimension=0, tiled=True),
    )
    token_count = block_in.shape[0] * lax.axis_size("dp") * lax.axis_size("row")
    factor = 1.0 / math.sqrt(token_count)
    grad_norm = grad_norm * factor
    grad_qkv = grad_qkv * factor
    grad_attn = grad_attn * factor
    grad_up = grad_up * factor
    grad_down = grad_down * factor
    new_norm, new_mom_norm = adam_step(norm_params, grad_norm, mom_norm, 0.0)
    new_qkv, new_mom_qkv = adam_step(w_qkv, grad_qkv, mom_qkv, decay_rate)
    new_attn, new_mom_attn = adam_step(w_attn, grad_attn, mom_attn, decay_rate)
    new_up, new_mom_up = adam_step(w_up, grad_up, mom_up, decay_rate)
    new_down, new_mom_down = adam_step(w_down, grad_down, mom_down, decay_rate)
    return (
        block_out,
        input_grad,
        grad_norm,
        grad_qkv,
        grad_attn,
        grad_up,
        grad_down,
        new_norm,
        new_qkv,
        new_attn,
        new_up,
        new_down,
        new_mom_norm,
        new_mom_qkv,
        new_mom_attn,
        new_mom_up,
        new_mom_down,
    )


def solution(mesh):
    in_specs = (
        P(("dp", "row"), "col"),
        P(("dp", "row"), "col"),
        P(None, "col"),
        P(None, "row", "dp", "col"),
        P("row", "dp", "col"),
        P(("dp", "row"), "col"),
        P(("dp", "row"), "col"),
        P(None, None, "col"),
        P(None, None, "row", "dp", "col"),
        P(None, "row", "dp", "col"),
        P(None, ("dp", "row"), "col"),
        P(None, ("dp", "row"), "col"),
    )
    out_specs = (
        P(("dp", "row"), "col"),
        P(("dp", "row"), "col"),
        P(None, "col"),
        P(None, "row", "dp", "col"),
        P("row", "dp", "col"),
        P(("dp", "row"), "col"),
        P(("dp", "row"), "col"),
        P(None, "col"),
        P(None, "row", "dp", "col"),
        P("row", "dp", "col"),
        P(("dp", "row"), "col"),
        P(("dp", "row"), "col"),
        P(None, None, "col"),
        P(None, None, "row", "dp", "col"),
        P(None, "row", "dp", "col"),
        P(None, ("dp", "row"), "col"),
        P(None, ("dp", "row"), "col"),
    )
    return jax.shard_map(
        on_device, mesh=mesh, in_specs=in_specs, out_specs=out_specs, check_vma=False
    )
```

profile of v0, /device:TPU:0, one launch (start us, length us, event | category | flops | bytes accessed | tf_op | source)
XLA Modules:
  0.0 679.9 jit_solution(14349840694385199696)
XLA Ops:
  9.3 2.6 psum.63
  13.3 2.5 psum.64
  19.0 13.0 %all_gather.36 = bf16[1024,384]{1,0:T(8,128)(2,1)S(1)} all-gather(bf16[512,384]{1,0:T(8,128)(2,1)S(1)} %add_convert_fusion.1), channel_id=1, replica_groups=mesh['dp'=8,'row'=2,'col'=2] {'row'}, dimensions={0}, use_global_device_ids=true | all-gather | bytes 1179648 | tf_op jit(solution)/shard_map/all_gather | solution.py:57
  32.0 33.5 %all_gather.37 = bf16[3,6,64,384]{3,2,1,0:T(8,128)(2,1)S(1)} all-gather(bf16[3,6,8,384]{3,2,1,0:T(8,128)(2,1)S(1)} %convert_element_type.60), channel_id=1, replica_groups=mesh['dp'=8,'row'=2,'col'=2] {'dp'}, dimensions={2}, use_global_device_ids=true | all-gather | bytes 995328 | tf_op jit(solution)/shard_map/all_gather | solution.py:170
  66.4 3.6 fusion.69
  71.9 31.2 %all_gather.39 = bf16[6,64,384]{2,1,0:T(8,128)(2,1)S(1)} all-gather(bf16[6,8,384]{2,1,0:T(8,128)(2,1)S(1)} %convert_element_type.65), channel_id=1, replica_groups=mesh['dp'=8,'row'=2,'col'=2] {'dp'}, dimensions={1}, use_global_device_ids=true | all-gather | bytes 331776 | tf_op jit(solution)/shard_map/all_gather | solution.py:171
  106.4 2.3 fusion.2
  111.4 2.8 convolution_convert_fusion.1
  114.2 2.5 all_gather.38
  119.5 17.4 %all_gather.44 = bf16[1024,384]{1,0:T(8,128)(2,1)S(1)} all-gather(bf16[512,384]{1,0:T(8,128)(2,1)S(1)} %convert_element_type.70), channel_id=1, replica_groups=mesh['dp'=8,'row'=2,'col'=2] {'row'}, dimensions={0}, use_global_device_ids=true | all-gather | bytes 1179648 | tf_op jit(solution)/shard_map/all_gather | solution.py:57
  136.8 6.0 fusion.73
  143.0 6.5 reduce-scatter.15.cloned.1.call-done
  150.8 2.5 psum.65
  153.5 2.5 psum.66
  156.2 24.1 %all_gather.40 = bf16[1024,384]{1,0:T(8,128)(2,1)} all-gather(bf16[512,384]{1,0:T(8,128)(2,1)S(1)} %add_convert_fusion), channel_id=1, replica_groups=mesh['dp'=8,'row'=2,'col'=2] {'row'}, dimensions={0}, use_global_device_ids=true | all-gather | bytes 1179648 | tf_op jit(solution)/shard_map/all_gather | solution.py:57
  180.3 5.9 fusion.71
  186.3 14.2 %reduce-scatter.17.cloned.1.call-done = f32[512,1536]{1,0:T(8,128)} async-done(((f32[1024,1536]{1,0:T(8,128)}), f32[512,1536]{1,0:T(8,128)}) %reduce-scatter.17.cloned.1.call-update) | async-done | bytes 3145744 | tf_op jit(solution)/shard_map/reduce_scatter | solution.py:59
  200.5 5.2 multiply_convert_fusion.1
  206.3 13.7 %all-gather.12.cloned.1.call-done = bf16[1024,1536]{1,0:T(8,128)(2,1)} async-done(((bf16[512,1536]{1,0:T(8,128)(2,1)}), bf16[1024,1536]{1,0:T(8,128)(2,1)}) %all-gather.12.cloned.1.call-update) | async-done | bytes 3145744 | tf_op jit(solution)/shard_map/all_gather | solution.py:72
  220.0 5.2 fusion.74
  225.3 9.4 %all-gather.8.cloned.1.call-done = bf16[1024,1536]{1,0:T(8,128)(2,1)} async-done(((bf16[512,1536]{1,0:T(8,128)(2,1)}), bf16[1024,1536]{1,0:T(8,128)(2,1)}) %all-gather.8.cloned.1.call-update) | async-done | bytes 3145744 | tf_op jit(solution)/shard_map/all_gather | solution.py:72
  234.7 5.1 fusion.72
  240.0 24.4 %reduce-scatter.23.cloned.1.call-done = f32[512,384]{1,0:T(8,128)} async-done(((f32[1024,384]{1,0:T(8,128)}), f32[512,384]{1,0:T(8,128)}) %reduce-scatter.23.cloned.1.call-update) | async-done | bytes 786448 | tf_op jit(solution)/shard_map/reduce_scatter | solution.py:74
  264.3 2.1 multiply_reduce_fusion.1
  266.5 2.4 all-reduce.1
  268.9 23.8 %reduce-scatter.19.cloned.1.call-done = f32[512,384]{1,0:T(8,128)} async-done(((f32[1024,384]{1,0:T(8,128)}), f32[512,384]{1,0:T(8,128)}) %reduce-scatter.19.cloned.1.call-update) | async-done | bytes 786448 | tf_op jit(solution)/shard_map/reduce_scatter | solution.py:74
  292.8 3.0 fusion.67
  295.8 11.3 %all_gather.46 = bf16[1024,384]{1,0:T(8,128)(2,1)S(1)} all-gather(bf16[512,384]{1,0:T(8,128)(2,1)S(1)} %get-tuple-element.70), channel_id=1, replica_groups=mesh['dp'=8,'row'=2,'col'=2] {'row'}, dimensions={0}, use_global_device_ids=true | all-gather | bytes 1179648 | tf_op jit(solution)/shard_map/all_gather | solution.py:57
  309.0 9.1 %reduce-scatter.25.cloned.1.call-done = f32[512,384]{1,0:T(8,128)} async-done(((f32[1024,384]{1,0:T(8,128)}), f32[512,384]{1,0:T(8,128)}) %reduce-scatter.25.cloned.1.call-update) | async-done | bytes 786448 | tf_op jit(solution)/shard_map/reduce_scatter | solution.py:59
  318.1 1.9 convert_element_type.73
  321.2 5.2 fusion.36
  326.4 4.7 fusion.43
  331.1 13.3 %fusion.40 = bf16[512,1,6,64]{0,3,2,1:T(8,128)(2,1)} fusion(f32[6,512,512]{1,2,0:T(8,128)} %fusion.43, f32[6,512,512]{1,2,0:T(8,128)} %copy-done.1, f32[6,512]{1,0:T(8,128)} %copy-done.28, pred[512,512]{0,1:T(8,128)(4,1)} %copy-done.17, bf16[512,3,6,64]{0,3,2,1:T(8,128)(2,1)} %bitcast.169), kind=kOutput, calls=%fused_computation.30 | convolution fusion | flops 218828288 | bytes 26509312 | tf_op jit(solution)/shard_map/while/body/eval_jaxpr/hqk,khd->qhd/dot_general | solution.py:132
  344.4 13.4 %fusion.37 = bf16[512,1,6,64]{0,3,2,1:T(8,128)(2,1)} fusion(f32[6,512,512]{1,2,0:T(8,128)} %fusion.43, f32[6,512,512]{1,2,0:T(8,128)} %copy-done.1, f32[6,512]{1,0:T(8,128)} %copy-done.28, pred[512,512]{0,1:T(8,128)(4,1)} %copy-done.17, bf16[512,3,6,64]{0,3,2,1:T(8,128)(2,1)} %bitcast.170), kind=kOutput, calls=%fused_computation.29 | convolution fusion | flops 218828288 | bytes 26509312 | tf_op jit(solution)/shard_map/while/body/eval_jaxpr/hqk,qhd->khd/dot_general | solution.py:135
  357.8 2.3 pad_maximum_fusion
  361.8 5.3 fusion.79
  367.2 5.6 fusion.80
  372.9 4.4 fusion.76
  377.4 4.4 fusion.77
  381.8 44.2 %reduce-scatter.31.cloned.1.call-done = f32[6,8,384]{2,1,0:T(8,128)} async-done(((f32[6,64,384]{2,1,0:T(8,128)}), f32[6,8,384]{2,1,0:T(8,128)}) %reduce-scatter.31.cloned.1.call-update) | async-done | bytes 73744 | tf_op jit(solution)/shard_map/reduce_scatter | solution.py:224
  429.2 69.5 %reduce-scatter.33.cloned.1.call-done = f32[192,384]{1,0:T(8,128)} async-done(((f32[1536,384]{1,0:T(8,128)}), f32[192,384]{1,0:T(8,128)}) %reduce-scatter.33.cloned.1.call-update) | async-done | bytes 294928 | tf_op jit(solution)/shard_map/reduce_scatter | solution.py:225
  500.7 70.5 %reduce-scatter.35.cloned.1.call-done = f32[192,384]{1,0:T(8,128)} async-done(((f32[1536,384]{1,0:T(8,128)}), f32[192,384]{1,0:T(8,128)}) %reduce-scatter.35.cloned.1.call-update) | async-done | bytes 294928 | tf_op jit(solution)/shard_map/reduce_scatter | solution.py:226
  575.2 2.0 multiply_subtract_fusion
  577.1 21.6 %reduce-scatter.27.cloned.1.call-done = f32[512,384]{1,0:T(8,128)} async-done(((f32[1024,384]{1,0:T(8,128)}), f32[512,384]{1,0:T(8,128)}) %reduce-scatter.27.cloned.1.call-update) | async-done | bytes 786448 | tf_op jit(solution)/shard_map/reduce_scatter | solution.py:74
  600.4 2.6 all-reduce
  603.0 41.8 %psum.71 = f32[4,384]{1,0:T(4,128)S(1)} all-reduce(f32[4,384]{1,0:T(4,128)S(1)} %pad_maximum_fusion.6), channel_id=1, replica_groups=mesh['dp'=8,'row'=2,'col'=2] {'dp','row'}, use_global_device_ids=true, to_apply=%region_31.32 | all-reduce | flops 1536 | bytes 12288 | tf_op jit(solution)/shard_map/psum | solution.py:221
  646.1 2.4 multiply_add_fusion.1
  648.5 19.9 %reduce-scatter.29.cloned.1.call-done = f32[3,6,8,384]{3,2,1,0:T(8,128)} async-done(((f32[3,6,64,384]{3,2,1,0:T(8,128)}), f32[3,6,8,384]{3,2,1,0:T(8,128)}) %reduce-scatter.29.cloned.1.call-update) | async-done | bytes 221200 | tf_op jit(solution)/shard_map/reduce_scatter | solution.py:223
  (147 shorter events, 40.5 us)
Async XLA Ops:
  8.0 95.0 %reduce-scatter.13.cloned.1.call-start = ((), (), s32[]{:S(2)}) async-start(), calls=%async_computation.12 | async-start | bytes 7077888 | tf_op jit(solution)/shard_map/reduce_scatter | solution.py:59
  65.5 0.9 copy-start.4
  70.0 1.0 copy-start.16
  70.0 1.8 copy-start.23
  70.1 66.8 %all-gather.10.cloned.1.call-start = ((), (), s32[]{:S(2)}) async-start(), calls=%async_computation.17 | async-start | bytes 1327104 | tf_op jit(solution)/shard_map/all_gather | solution.py:173
  71.7 77.8 %reduce-scatter.15.cloned.1.call-start = ((), (), s32[]{:S(2)}) async-start(), calls=%async_computation.13 | async-start | bytes 2359296 | tf_op jit(solution)/shard_map/reduce_scatter | solution.py:74
  71.8 38.2 %copy-start.17 = (pred[512,512]{0,1:T(8,128)(4,1)}, pred[512,512]{0,1:T(8,128)(4,1)S(1)}, u32[]{:S(2)}) copy-start(pred[512,512]{0,1:T(8,128)(4,1)S(1)} %iota_compare_fusion) | copy-start | bytes 786436
  108.7 2.7 copy-start.1
  111.3 2.8 copy-start.28
  114.1 4.5 copy-start.15
  114.2 5.2 copy-start.6
  118.6 61.7 %all-gather.6.cloned.1.call-start = ((), (), s32[]{:S(2)}) async-start(), calls=%async_computation.14 | async-start | bytes 1327104 | tf_op jit(solution)/shard_map/all_gather | solution.py:172
  119.3 67.0 %reduce-scatter.21.cloned.1.call-start = ((), (), s32[]{:S(2)}) async-start(), calls=%async_computation.19 | async-start | bytes 9437184 | tf_op jit(solution)/shard_map/reduce_scatter | solution.py:59
  136.8 6.0 copy-start.2
  142.9 6.6 copy-start
  142.9 57.6 %reduce-scatter.17.cloned.1.call-start = ((), (), s32[]{:S(2)}) async-start(), calls=%async_computation.15 | async-start | bytes 9437184 | tf_op jit(solution)/shard_map/reduce_scatter | solution.py:59
  186.3 33.8 %all-gather.12.cloned.1.call-start = ((), (), s32[]{:S(2)}) async-start(), calls=%async_computation.20 | async-start | bytes 4718592 | tf_op jit(solution)/shard_map/all_gather | solution.py:72
  205.7 29.0 %all-gather.8.cloned.1.call-start = ((), (), s32[]{:S(2)}) async-start(), calls=%async_computation.16 | async-start | bytes 4718592 | tf_op jit(solution)/shard_map/all_gather | solution.py:72
  206.3 58.1 %reduce-scatter.23.cloned.1.call-start = ((), (), s32[]{:S(2)}) async-start(), calls=%async_computation.21 | async-start | bytes 2359296 | tf_op jit(solution)/shard_map/reduce_scatter | solution.py:74
  225.3 67.5 %reduce-scatter.19.cloned.1.call-start = ((), (), s32[]{:S(2)}) async-start(), calls=%async_computation.18 | async-start | bytes 2359296 | tf_op jit(solution)/shard_map/reduce_scatter | solution.py:74
  239.9 78.2 %reduce-scatter.25.cloned.1.call-start = ((), (), s32[]{:S(2)}) async-start(), calls=%async_computation.22 | async-start | bytes 2359296 | tf_op jit(solution)/shard_map/reduce_scatter | solution.py:59
  308.9 63.9 %all-gather.14.cloned.1.call-start = ((), (), s32[]{:S(2)}) async-start(), calls=%async_computation.23 | async-start | bytes 3538944 | tf_op jit(solution)/shard_map/all_gather | solution.py:72
  344.4 13.4 %copy-start.21 = (bf16[512,1,6,64]{0,3,2,1:T(8,128)(2,1)S(1)}, bf16[512,1,6,64]{0,3,2,1:T(8,128)(2,1)}, u32[]{:S(2)}) copy-start(bf16[512,1,6,64]{0,3,2,1:T(8,128)(2,1)} %fusion.36) | copy-start | bytes 1179652
  360.0 65.9 %reduce-scatter.31.cloned.1.call-start = ((), (), s32[]{:S(2)}) async-start(), calls=%async_computation.26 | async-start | bytes 663552 | tf_op jit(solution)/shard_map/reduce_scatter | solution.py:224
  361.5 5.7 copy-start.3
  361.5 137.2 %reduce-scatter.33.cloned.1.call-start = ((), (), s32[]{:S(2)}) async-start(), calls=%async_computation.27 | async-start | bytes 2654208 | tf_op jit(solution)/shard_map/reduce_scatter | solution.py:225
  367.1 5.8 copy-start.5
  367.1 204.1 %reduce-scatter.35.cloned.1.call-start = ((), (), s32[]{:S(2)}) async-start(), calls=%async_computation.28 | async-start | bytes 2654208 | tf_op jit(solution)/shard_map/reduce_scatter | solution.py:226
  372.8 226.0 %reduce-scatter.27.cloned.1.call-start = ((), (), s32[]{:S(2)}) async-start(), calls=%async_computation.24 | async-start | bytes 2359296 | tf_op jit(solution)/shard_map/reduce_scatter | solution.py:74
  377.3 4.5 copy-start.29
  377.3 48.7 %copy-start.20 = (f32[2,6,8,384]{3,2,1,0:T(8,128)S(1)}, f32[2,6,8,384]{3,2,1,0:T(8,128)}, u32[]{:S(2)}) copy-start(f32[2,6,8,384]{3,2,1,0:T(8,128)} %param.21) | copy-start | bytes 442372
  377.3 50.3 %copy-start.24 = (f32[6,8,384]{2,1,0:T(8,128)S(1)}, f32[6,8,384]{2,1,0:T(8,128)}, u32[]{:S(2)}) copy-start(f32[6,8,384]{2,1,0:T(8,128)} %param.16) | copy-start | bytes 221188
  377.3 291.1 %reduce-scatter.29.cloned.1.call-start = ((), (), s32[]{:S(2)}) async-start(), calls=%async_computation.25 | async-start | bytes 1990656 | tf_op jit(solution)/shard_map/reduce_scatter | solution.py:223
  381.7 117.0 %copy-start.8 = (f32[2,192,384]{2,1,0:T(8,128)S(1)}, f32[2,192,384]{2,1,0:T(8,128)}, u32[]{:S(2)}) copy-start(f32[2,192,384]{2,1,0:T(8,128)} %param.22) | copy-start | bytes 1769476
  381.7 189.4 %copy-start.9 = (f32[2,192,384]{2,1,0:T(8,128)S(1)}, f32[2,192,384]{2,1,0:T(8,128)}, u32[]{:S(2)}) copy-start(f32[2,192,384]{2,1,0:T(8,128)} %param.23) | copy-start | bytes 1769476
  426.9 146.3 %copy-start.22 = (f32[6,8,384]{2,1,0:T(8,128)}, f32[6,8,384]{2,1,0:T(8,128)S(1)}, u32[]{:S(2)}) copy-start(f32[6,8,384]{2,1,0:T(8,128)S(1)} %get-tuple-element.65) | copy-start | bytes 221188
  499.8 77.4 %copy-start.11 = (f32[192,384]{1,0:T(8,128)}, f32[192,384]{1,0:T(8,128)S(1)}, u32[]{:S(2)}) copy-start(f32[192,384]{1,0:T(8,128)S(1)} %get-tuple-element.63) | copy-start | bytes 884740
  571.2 2.1 copy-start.13
  571.2 4.0 copy-start.14
  572.3 28.0 %copy-start.12 = (f32[192,384]{1,0:T(8,128)}, f32[192,384]{1,0:T(8,128)S(1)}, u32[]{:S(2)}) copy-start(f32[192,384]{1,0:T(8,128)S(1)} %get-tuple-element.61) | copy-start | bytes 884740
  572.3 72.5 %copy-start.25 = (f32[2,4,384]{2,1,0:T(4,128)S(1)}, f32[2,4,384]{2,1,0:T(4,128)}, u32[]{:S(2)}) copy-start(f32[2,4,384]{2,1,0:T(4,128)} %param.19) | copy-start | bytes 36868
  572.4 73.1 %copy-start.26 = (f32[4,384]{1,0:T(4,128)S(1)}, f32[4,384]{1,0:T(4,128)}, u32[]{:S(2)}) copy-start(f32[4,384]{1,0:T(4,128)} %param.14) | copy-start | bytes 18436
  572.4 73.8 %copy-start.7 = (f32[512,384]{1,0:T(8,128)S(1)}, f32[512,384]{1,0:T(8,128)}, u32[]{:S(2)}) copy-start(f32[512,384]{1,0:T(8,128)} %get-tuple-element.71) | copy-start | bytes 2359300
  575.2 93.2 %copy-start.10 = (f32[2,3,6,8,384]{4,3,2,1,0:T(8,128)S(1)}, f32[2,3,6,8,384]{4,3,2,1,0:T(8,128)}, u32[]{:S(2)}) copy-start(f32[2,3,6,8,384]{4,3,2,1,0:T(8,128)} %param.20) | copy-start | bytes 1327108
  600.3 69.9 %copy-start.18 = (f32[3,6,8,384]{3,2,1,0:T(8,128)S(1)}, f32[3,6,8,384]{3,2,1,0:T(8,128)}, u32[]{:S(2)}) copy-start(f32[3,6,8,384]{3,2,1,0:T(8,128)} %param.15) | copy-start | bytes 663556
  644.9 27.2 %copy-start.27 = (f32[4,384]{1,0:T(4,128)}, f32[4,384]{1,0:T(4,128)S(1)}, u32[]{:S(2)}) copy-start(f32[4,384]{1,0:T(4,128)S(1)} %get-tuple-element.69) | copy-start | bytes 18436
  669.4 2.6 copy-start.19
Sparse Core Ops, SparseCore 0:
  70.2 12.6 reduce-scatter.12
  118.7 30.7 reduce-scatter.14
  151.8 14.0 reduce-scatter.20
  186.4 14.0 reduce-scatter.16
  205.8 14.1 all-gather.11
  221.4 13.2 all-gather.7
  237.0 27.3 reduce-scatter.22
  266.6 26.1 reduce-scatter.18
  309.1 9.0 reduce-scatter.24
  360.2 12.2 all-gather.13
Sparse Core Ops, SparseCore 1:
  73.3 41.7 all-gather.9
  121.8 41.2 all-gather.5
  364.4 61.5 reduce-scatter.30
  429.5 69.1 reduce-scatter.32
  502.2 68.9 reduce-scatter.34
  573.5 25.3 reduce-scatter.26
  602.1 66.2 reduce-scatter.28
where the time goes:
time: 689 us; the launch traced here: 680 us
  waiting for transfers between devices  328 us (48%)
  blocking collectives  190 us (28%)
  matrix products  92.3 us (13%)
  other arithmetic  45.7 us (7%)
  between operations  16.5 us (2%)
    reduce_scatter x4, waiting for transfers between devices, cols_then_rows(): lax.psum_scatter(jnp.dot(everyone, weight, preferred_element_type=jnp.flo...  76.4 us
    reduce_scatter x1, waiting for transfers between devices, on_device(): lax.psum_scatter(grad_down, 'dp', scatter_dimension=0, tiled=True)  70.5 us
    reduce_scatter x1, waiting for transfers between devices, on_device(): lax.psum_scatter(grad_up, 'dp', scatter_dimension=0, tiled=True)  69.5 us
    all_gather x4, blocking collectives, rows_then_cols(): everyone = lax.all_gather(local_rows, 'row', axis=0, tiled=True)  65.7 us
    reduce_scatter x1, waiting for transfers between devices, on_device(): lax.psum_scatter(grad_attn, 'dp', scatter_dimension=1, tiled=True)  44.2 us
    psum x1, blocking collectives, on_device(): grad_norm, = lax.psum((norm_terms,), ('dp', 'row'))  41.8 us
    all_gather x1, blocking collectives, on_device(): lax.all_gather(w_qkv.astype(jnp.bfloat16), 'dp', axis=2, tiled=True)  33.5 us
    all_gather x1, blocking collectives, on_device(): lax.all_gather(w_attn.astype(jnp.bfloat16), 'dp', axis=1, tiled=True)  31.2 us
  transfers between devices with their start and end apart: 17, of which 12 were waited for; matrix products, arithmetic and copies ran while one was open for 11% of the time, Pallas kernels for 0%

commit v1 on v0

--- a/solution.py
+++ b/solution.py
@@ -54,7 +54,14 @@
 
 
 def rows_then_cols(local_rows, weight):
-    everyone = lax.all_gather(local_rows, "row", axis=0, tiled=True)
+    ways, here = (lax.axis_size("row"), lax.axis_index("row"))
+    everyone, reach = (local_rows, 1)
+    while reach < ways:
+        theirs = lax.ppermute(everyone, "row", [(d, d ^ reach) for d in range(ways)])
+        mine_first = jnp.concatenate([everyone, theirs], axis=0)
+        theirs_first = jnp.concatenate([theirs, everyone], axis=0)
+        everyone = jnp.where(here & reach == 0, mine_first, theirs_first)
+        reach = 2 * reach
     return (
         lax.psum_scatter(
             lax.dot_general(

time: 689 us -> 654 us (0.949); the launches traced: 680 us -> 653 us
  blocking collectives: 190 us -> 125 us
  waiting for transfers between devices: 328 us -> 361 us
    all_gather x4 -> x0, blocking collectives: 65.7 us -> none  [rows_then_cols(): everyone = lax.all_gather(local_rows, 'row', axis=0, tiled=True)]
    ppermute x0 -> x4, waiting for transfers between devices: none -> 32.5 us  [rows_then_cols(): lax.ppermute(everyone, 'row', [(d, d ^ reach) for d in range(ways)])]
  transfers between devices with their start and end apart: 17 -> 21, of which waited for: 12 -> 16; matrix products, arithmetic and copies ran while one was open for 11% -> 13% of each run, Pallas kernels for 0% -> 0%
where the time goes in v1:
time: 654 us; the launch traced here: 653 us
  waiting for transfers between devices  361 us (55%)
  blocking collectives  125 us (19%)
  matrix products  90.6 us (14%)
  other arithmetic  48.4 us (7%)
  between operations  16.3 us (2%)
    reduce_scatter x4, waiting for transfers between devices, cols_then_rows(): lax.psum_scatter(jnp.dot(everyone, weight, preferred_element_type=jnp.flo...  73.7 us
    reduce_scatter x1, waiting for transfers between devices, on_device(): lax.psum_scatter(grad_up, 'dp', scatter_dimension=0, tiled=True)  70.7 us
    reduce_scatter x1, waiting for transfers between devices, on_device(): lax.psum_scatter(grad_down, 'dp', scatter_dimension=0, tiled=True)  70.5 us
    reduce_scatter x1, waiting for transfers between devices, on_device(): lax.psum_scatter(grad_attn, 'dp', scatter_dimension=1, tiled=True)  42.8 us
    psum x1, blocking collectives, on_device(): grad_norm, = lax.psum((norm_terms,), ('dp', 'row'))  42 us
    all_gather x1, blocking collectives, on_device(): lax.all_gather(w_qkv.astype(jnp.bfloat16), 'dp', axis=2, tiled=True)  32.7 us
    ppermute x4, waiting for transfers between devices, rows_then_cols(): lax.ppermute(everyone, 'row', [(d, d ^ reach) for d in range(ways)])  32.5 us
    all_gather x1, blocking collectives, on_device(): lax.all_gather(w_attn.astype(jnp.bfloat16), 'dp', axis=1, tiled=True)  31.2 us
  transfers between devices with their start and end apart: 21, of which 16 were waited for; matrix products, arithmetic and copies ran while one was open for 13% of the time, Pallas kernels for 0%

profile of v1, /device:TPU:0, one launch (start us, length us, event | category | flops | bytes accessed | tf_op | source)
XLA Modules:
  0.0 652.8 jit_solution(8411115559810174437)
XLA Ops:
  9.3 2.6 psum.63
  13.3 2.5 psum.64
  18.7 2.9 collective-permute-start
  22.5 32.7 %all_gather.24 = bf16[3,6,64,384]{3,2,1,0:T(8,128)(2,1)S(1)} all-gather(bf16[3,6,8,384]{3,2,1,0:T(8,128)(2,1)S(1)} %convert_element_type.60), channel_id=1, replica_groups=mesh['dp'=8,'row'=2,'col'=2] {'dp'}, dimensions={2}, use_global_device_ids=true | all-gather | bytes 995328 | tf_op jit(solution)/shard_map/all_gather | solution.py:177
  55.2 3.6 fusion.50
  60.7 31.2 %all_gather.26 = bf16[6,64,384]{2,1,0:T(8,128)(2,1)S(1)} all-gather(bf16[6,8,384]{2,1,0:T(8,128)(2,1)S(1)} %convert_element_type.65), channel_id=1, replica_groups=mesh['dp'=8,'row'=2,'col'=2] {'dp'}, dimensions={1}, use_global_device_ids=true | all-gather | bytes 331776 | tf_op jit(solution)/shard_map/all_gather | solution.py:178
  95.2 2.3 fusion.2
  100.2 2.8 convolution_convert_fusion.1
  103.0 2.5 all_gather.25
  108.9 15.3 %collective-permute-done.2 = bf16[512,384]{1,0:T(8,128)(2,1)S(1)} collective-permute-done((bf16[512,384]{1,0:T(8,128)(2,1)S(1)}, bf16[512,384]{1,0:T(8,128)(2,1)S(1)}, u32[]{:S(2)}, u32[]{:S(2)}) %collective-permute-start.2) | collective-permute-done | bytes 393248 | tf_op jit(solution)/shard_map/ppermute | solution.py:60
  124.2 5.9 fusion.46
  130.2 7.5 %reduce-scatter.15.cloned.1.call-done = f32[512,384]{1,0:T(8,128)} async-done(((f32[1024,384]{1,0:T(8,128)}), f32[512,384]{1,0:T(8,128)}) %reduce-scatter.15.cloned.1.call-update) | async-done | bytes 786448 | tf_op jit(solution)/shard_map/reduce_scatter | solution.py:81
  139.1 2.5 psum.65
  141.8 3.2 psum.66
  147.8 4.2 all-gather.6.cloned.1.call-done
  152.1 6.8 %collective-permute-done.1 = bf16[512,384]{1,0:T(8,128)(2,1)} collective-permute-done((bf16[512,384]{1,0:T(8,128)(2,1)}, bf16[512,384]{1,0:T(8,128)(2,1)}, u32[]{:S(2)}, u32[]{:S(2)}) %collective-permute-start.1) | collective-permute-done | bytes 393248 | tf_op jit(solution)/shard_map/ppermute | solution.py:60
  158.8 6.2 fusion.48
  165.1 14.3 %reduce-scatter.17.cloned.1.call-done = f32[512,1536]{1,0:T(8,128)} async-done(((f32[1024,1536]{1,0:T(8,128)}), f32[512,1536]{1,0:T(8,128)}) %reduce-scatter.17.cloned.1.call-update) | async-done | bytes 3145744 | tf_op jit(solution)/shard_map/reduce_scatter | solution.py:66
  179.4 5.2 multiply_convert_fusion.1
  185.2 13.7 %all-gather.12.cloned.1.call-done = bf16[1024,1536]{1,0:T(8,128)(2,1)} async-done(((bf16[512,1536]{1,0:T(8,128)(2,1)}), bf16[1024,1536]{1,0:T(8,128)(2,1)}) %all-gather.12.cloned.1.call-update) | async-done | bytes 3145744 | tf_op jit(solution)/shard_map/all_gather | solution.py:79
  198.9 5.2 fusion.87
  204.2 9.4 %all-gather.8.cloned.1.call-done = bf16[1024,1536]{1,0:T(8,128)(2,1)} async-done(((bf16[512,1536]{1,0:T(8,128)(2,1)}), bf16[1024,1536]{1,0:T(8,128)(2,1)}) %all-gather.8.cloned.1.call-update) | async-done | bytes 3145744 | tf_op jit(solution)/shard_map/all_gather | solution.py:79
  213.6 5.1 fusion.86
  218.9 24.4 %reduce-scatter.23.cloned.1.call-done = f32[512,384]{1,0:T(8,128)} async-done(((f32[1024,384]{1,0:T(8,128)}), f32[512,384]{1,0:T(8,128)}) %reduce-scatter.23.cloned.1.call-update) | async-done | bytes 786448 | tf_op jit(solution)/shard_map/reduce_scatter | solution.py:81
  243.2 2.2 multiply_reduce_fusion.1
  245.4 3.1 all-reduce.1
  249.8 21.9 %reduce-scatter.19.cloned.1.call-done = f32[512,384]{1,0:T(8,128)} async-done(((f32[1024,384]{1,0:T(8,128)}), f32[512,384]{1,0:T(8,128)}) %reduce-scatter.19.cloned.1.call-update) | async-done | bytes 786448 | tf_op jit(solution)/shard_map/reduce_scatter | solution.py:81
  271.7 2.8 fusion.83
  274.8 10.3 %collective-permute-done.3 = bf16[512,384]{1,0:T(8,128)(2,1)S(1)} collective-permute-done((bf16[512,384]{1,0:T(8,128)(2,1)S(1)}, bf16[512,384]{1,0:T(8,128)(2,1)S(1)}, u32[]{:S(2)}, u32[]{:S(2)}) %collective-permute-start.3) | collective-permute-done | bytes 393248 | tf_op jit(solution)/shard_map/ppermute | solution.py:60
  288.1 8.9 %reduce-scatter.25.cloned.1.call-done = f32[512,384]{1,0:T(8,128)} async-done(((f32[1024,384]{1,0:T(8,128)}), f32[512,384]{1,0:T(8,128)}) %reduce-scatter.25.cloned.1.call-update) | async-done | bytes 786448 | tf_op jit(solution)/shard_map/reduce_scatter | solution.py:66
  298.4 5.3 fusion.36
  303.7 3.7 fusion.43
  307.4 13.1 %fusion.40 = bf16[512,1,6,64]{0,3,2,1:T(8,128)(2,1)} fusion(f32[6,512,512]{1,2,0:T(8,128)} %fusion.43, f32[6,512,512]{1,2,0:T(8,128)} %copy-done.1, f32[6,512]{1,0:T(8,128)S(1)} %copy-done.42, pred[512,512]{0,1:T(8,128)(4,1)} %copy-done.20, bf16[512,3,6,64]{0,3,2,1:T(8,128)(2,1)S(1)} %bitcast.158), kind=kOutput, calls=%fused_computation.30 | convolution fusion | flops 218828288 | bytes 26509312 | tf_op jit(solution)/shard_map/while/body/eval_jaxpr/hqk,khd->qhd/dot_general | solution.py:139
  320.4 11.3 %fusion.37 = bf16[512,1,6,64]{0,3,2,1:T(8,128)(2,1)} fusion(f32[6,512,512]{1,2,0:T(8,128)} %fusion.43, f32[6,512,512]{1,2,0:T(8,128)} %copy-done.1, f32[6,512]{1,0:T(8,128)S(1)} %copy-done.42, pred[512,512]{0,1:T(8,128)(4,1)} %copy-done.20, bf16[512,3,6,64]{0,3,2,1:T(8,128)(2,1)S(1)} %bitcast.159), kind=kOutput, calls=%fused_computation.29 | convolution fusion | flops 218828288 | bytes 26509312 | tf_op jit(solution)/shard_map/while/body/eval_jaxpr/hqk,qhd->khd/dot_general | solution.py:142
  331.7 2.3 pad_maximum_fusion
  334.2 2.5 fusion.51
  336.8 5.6 fusion.47
  342.7 5.4 fusion.45
  348.3 4.4 fusion.88
  352.8 4.5 fusion.49
  357.4 42.8 %reduce-scatter.31.cloned.1.call-done = f32[6,8,384]{2,1,0:T(8,128)} async-done(((f32[6,64,384]{2,1,0:T(8,128)}), f32[6,8,384]{2,1,0:T(8,128)}) %reduce-scatter.31.cloned.1.call-update) | async-done | bytes 73744 | tf_op jit(solution)/shard_map/reduce_scatter | solution.py:231
  401.8 70.7 %reduce-scatter.33.cloned.1.call-done = f32[192,384]{1,0:T(8,128)} async-done(((f32[1536,384]{1,0:T(8,128)}), f32[192,384]{1,0:T(8,128)}) %reduce-scatter.33.cloned.1.call-update) | async-done | bytes 294928 | tf_op jit(solution)/shard_map/reduce_scatter | solution.py:232
  474.5 70.5 %reduce-scatter.35.cloned.1.call-done = f32[192,384]{1,0:T(8,128)} async-done(((f32[1536,384]{1,0:T(8,128)}), f32[192,384]{1,0:T(8,128)}) %reduce-scatter.35.cloned.1.call-update) | async-done | bytes 294928 | tf_op jit(solution)/shard_map/reduce_scatter | solution.py:233
  552.6 19.9 %reduce-scatter.27.cloned.1.call-done = f32[512,384]{1,0:T(8,128)} async-done(((f32[1024,384]{1,0:T(8,128)}), f32[512,384]{1,0:T(8,128)}) %reduce-scatter.27.cloned.1.call-update) | async-done | bytes 786448 | tf_op jit(solution)/shard_map/reduce_scatter | solution.py:81
  574.1 2.6 all-reduce
  576.7 42.0 %psum.71 = f32[4,384]{1,0:T(4,128)S(1)} all-reduce(f32[4,384]{1,0:T(4,128)S(1)} %pad_maximum_fusion.6), channel_id=1, replica_groups=mesh['dp'=8,'row'=2,'col'=2] {'dp','row'}, use_global_device_ids=true, to_apply=%region_31.32 | all-reduce | flops 1536 | bytes 12288 | tf_op jit(solution)/shard_map/psum | solution.py:228
  620.0 2.4 multiply_add_fusion.1
  622.4 19.4 %reduce-scatter.29.cloned.1.call-done = f32[3,6,8,384]{3,2,1,0:T(8,128)} async-done(((f32[3,6,64,384]{3,2,1,0:T(8,128)}), f32[3,6,8,384]{3,2,1,0:T(8,128)}) %reduce-scatter.29.cloned.1.call-update) | async-done | bytes 221200 | tf_op jit(solution)/shard_map/reduce_scatter | solution.py:230
  (183 shorter events, 47.0 us)
Async XLA Ops:
  8.0 83.9 %reduce-scatter.13.cloned.1.call-start = ((), (), s32[]{:S(2)}) async-start(), calls=%async_computation.12 | async-start | bytes 7077888 | tf_op jit(solution)/shard_map/reduce_scatter | solution.py:66
  15.8 5.7 copy-start.37
  18.6 40.2 %copy-start.12 = (bf16[512,384]{1,0:T(8,128)(2,1)}, bf16[512,384]{1,0:T(8,128)(2,1)S(1)}, u32[]{:S(2)}) copy-start(bf16[512,384]{1,0:T(8,128)(2,1)S(1)} %add_convert_fusion.1) | copy-start | bytes 1179652
  18.7 36.6 %collective-permute-start = (bf16[512,384]{1,0:T(8,128)(2,1)S(1)}, bf16[512,384]{1,0:T(8,128)(2,1)S(1)}, u32[]{:S(2)}, u32[]{:S(2)}) collective-permute-start(bf16[512,384]{1,0:T(8,128)(2,1)S(1)} %add_convert_fusion.1), channel_id=1, source_target_pairs={{0,2},{2,0},{1,3},{3,1},{4,6},{6,4},{5,7},{7,5},{8,10},{10,8},{9,1... | collective-permute-start | bytes 1179656 | tf_op jit(solution)/shard_map/ppermute | solution.py:60
  58.9 65.3 %all-gather.10.cloned.1.call-start = ((), (), s32[]{:S(2)}) async-start(), calls=%async_computation.17 | async-start | bytes 1327104 | tf_op jit(solution)/shard_map/all_gather | solution.py:180
  60.5 77.3 %reduce-scatter.15.cloned.1.call-start = ((), (), s32[]{:S(2)}) async-start(), calls=%async_computation.13 | async-start | bytes 2359296 | tf_op jit(solution)/shard_map/reduce_scatter | solution.py:81
  60.6 38.3 %copy-start.20 = (pred[512,512]{0,1:T(8,128)(4,1)}, pred[512,512]{0,1:T(8,128)(4,1)S(1)}, u32[]{:S(2)}) copy-start(pred[512,512]{0,1:T(8,128)(4,1)S(1)} %iota_compare_fusion) | copy-start | bytes 786436
  105.5 24.6 %copy-start.4 = (bf16[1024,384]{0,1:T(8,128)(2,1)}, bf16[1024,384]{0,1:T(8,128)(2,1)S(1)}, u32[]{:S(2)}) copy-start(bf16[1024,384]{0,1:T(8,128)(2,1)S(1)} %all_gather.25) | copy-start | bytes 2359300
  107.4 44.6 %all-gather.6.cloned.1.call-start = ((), (), s32[]{:S(2)}) async-start(), calls=%async_computation.14 | async-start | bytes 1327104 | tf_op jit(solution)/shard_map/all_gather | solution.py:179
  108.2 56.9 %reduce-scatter.21.cloned.1.call-start = ((), (), s32[]{:S(2)}) async-start(), calls=%async_computation.19 | async-start | bytes 9437184 | tf_op jit(solution)/shard_map/reduce_scatter | solution.py:66
  108.3 21.8 %copy-start.10 = (bf16[512,384]{1,0:T(8,128)(2,1)}, bf16[512,384]{1,0:T(8,128)(2,1)S(1)}, u32[]{:S(2)}) copy-start(bf16[512,384]{1,0:T(8,128)(2,1)S(1)} %convert_element_type.70) | copy-start | bytes 1179652
  108.3 15.9 %collective-permute-start.2 = (bf16[512,384]{1,0:T(8,128)(2,1)S(1)}, bf16[512,384]{1,0:T(8,128)(2,1)S(1)}, u32[]{:S(2)}, u32[]{:S(2)}) collective-permute-start(bf16[512,384]{1,0:T(8,128)(2,1)S(1)} %convert_element_type.70), channel_id=1, source_target_pairs={{0,2},{2,0},{1,3},{3,1},{4,6},{6,4},{5,7},{7,5},{8,10},{10,8},{9,1... | collective-permute-start | bytes 1179656 | tf_op jit(solution)/shard_map/ppermute | solution.py:60
  124.2 5.9 copy-start.24
  130.1 7.6 %copy-start = (f32[512,384]{1,0:T(8,128)S(1)}, f32[512,384]{1,0:T(8,128)}, u32[]{:S(2)}) copy-start(f32[512,384]{1,0:T(8,128)} %param.12) | copy-start | bytes 2359300
  130.2 49.2 %reduce-scatter.17.cloned.1.call-start = ((), (), s32[]{:S(2)}) async-start(), calls=%async_computation.15 | async-start | bytes 9437184 | tf_op jit(solution)/shard_map/reduce_scatter | solution.py:66
  147.3 11.5 %collective-permute-start.1 = (bf16[512,384]{1,0:T(8,128)(2,1)}, bf16[512,384]{1,0:T(8,128)(2,1)}, u32[]{:S(2)}, u32[]{:S(2)}) collective-permute-start(bf16[512,384]{1,0:T(8,128)(2,1)} %add_convert_fusion), channel_id=1, source_target_pairs={{0,2},{2,0},{1,3},{3,1},{4,6},{6,4},{5,7},{7,5},{8,10},{10,8},{9,1... | collective-permute-start | bytes 1179656 | tf_op jit(solution)/shard_map/ppermute | solution.py:60
  165.1 33.8 %all-gather.12.cloned.1.call-start = ((), (), s32[]{:S(2)}) async-start(), calls=%async_computation.20 | async-start | bytes 4718592 | tf_op jit(solution)/shard_map/all_gather | solution.py:79
  184.6 29.0 %all-gather.8.cloned.1.call-start = ((), (), s32[]{:S(2)}) async-start(), calls=%async_computation.16 | async-start | bytes 4718592 | tf_op jit(solution)/shard_map/all_gather | solution.py:79
  185.2 58.0 %reduce-scatter.23.cloned.1.call-start = ((), (), s32[]{:S(2)}) async-start(), calls=%async_computation.21 | async-start | bytes 2359296 | tf_op jit(solution)/shard_map/reduce_scatter | solution.py:81
  204.2 67.5 %reduce-scatter.19.cloned.1.call-start = ((), (), s32[]{:S(2)}) async-start(), calls=%async_computation.18 | async-start | bytes 2359296 | tf_op jit(solution)/shard_map/reduce_scatter | solution.py:81
  218.8 78.2 %reduce-scatter.25.cloned.1.call-start = ((), (), s32[]{:S(2)}) async-start(), calls=%async_computation.22 | async-start | bytes 2359296 | tf_op jit(solution)/shard_map/reduce_scatter | solution.py:66
  274.5 10.7 %copy-start.28 = (bf16[512,384]{1,0:T(8,128)(2,1)}, bf16[512,384]{1,0:T(8,128)(2,1)S(1)}, u32[]{:S(2)}) copy-start(bf16[512,384]{1,0:T(8,128)(2,1)S(1)} %get-tuple-element.70) | copy-start | bytes 1179652
  274.5 10.7 %collective-permute-start.3 = (bf16[512,384]{1,0:T(8,128)(2,1)S(1)}, bf16[512,384]{1,0:T(8,128)(2,1)S(1)}, u32[]{:S(2)}, u32[]{:S(2)}) collective-permute-start(bf16[512,384]{1,0:T(8,128)(2,1)S(1)} %get-tuple-element.70), channel_id=1, source_target_pairs={{0,2},{2,0},{1,3},{3,1},{4,6},{6,4},{5,7},{7,5},{8,10},{10,8},{9,1... | collective-permute-start | bytes 1179656 | tf_op jit(solution)/shard_map/ppermute | solution.py:60
  287.8 60.5 %all-gather.14.cloned.1.call-start = ((), (), s32[]{:S(2)}) async-start(), calls=%async_computation.23 | async-start | bytes 3538944 | tf_op jit(solution)/shard_map/all_gather | solution.py:79
  320.4 11.3 %copy-start.30 = (bf16[512,1,6,64]{0,3,2,1:T(8,128)(2,1)S(1)}, bf16[512,1,6,64]{0,3,2,1:T(8,128)(2,1)}, u32[]{:S(2)}) copy-start(bf16[512,1,6,64]{0,3,2,1:T(8,128)(2,1)} %fusion.36) | copy-start | bytes 1179652
  334.1 66.0 %reduce-scatter.31.cloned.1.call-start = ((), (), s32[]{:S(2)}) async-start(), calls=%async_computation.26 | async-start | bytes 663552 | tf_op jit(solution)/shard_map/reduce_scatter | solution.py:231
  336.7 6.0 copy-start.11
  336.7 6.0 copy-start.25
  336.7 135.7 %reduce-scatter.33.cloned.1.call-start = ((), (), s32[]{:S(2)}) async-start(), calls=%async_computation.27 | async-start | bytes 2654208 | tf_op jit(solution)/shard_map/reduce_scatter | solution.py:232
  342.4 202.5 %reduce-scatter.35.cloned.1.call-start = ((), (), s32[]{:S(2)}) async-start(), calls=%async_computation.28 | async-start | bytes 2654208 | tf_op jit(solution)/shard_map/reduce_scatter | solution.py:233
  348.2 224.3 %reduce-scatter.27.cloned.1.call-start = ((), (), s32[]{:S(2)}) async-start(), calls=%async_computation.24 | async-start | bytes 2359296 | tf_op jit(solution)/shard_map/reduce_scatter | solution.py:81
  352.8 47.4 %copy-start.23 = (f32[2,6,8,384]{3,2,1,0:T(8,128)S(1)}, f32[2,6,8,384]{3,2,1,0:T(8,128)}, u32[]{:S(2)}) copy-start(f32[2,6,8,384]{3,2,1,0:T(8,128)} %param.21) | copy-start | bytes 442372
  352.8 119.7 %copy-start.6 = (f32[2,192,384]{2,1,0:T(8,128)S(1)}, f32[2,192,384]{2,1,0:T(8,128)}, u32[]{:S(2)}) copy-start(f32[2,192,384]{2,1,0:T(8,128)} %param.22) | copy-start | bytes 1769476
  352.8 288.9 %reduce-scatter.29.cloned.1.call-start = ((), (), s32[]{:S(2)}) async-start(), calls=%async_computation.25 | async-start | bytes 1990656 | tf_op jit(solution)/shard_map/reduce_scatter | solution.py:230
  357.3 187.6 %copy-start.7 = (f32[2,192,384]{2,1,0:T(8,128)S(1)}, f32[2,192,384]{2,1,0:T(8,128)}, u32[]{:S(2)}) copy-start(f32[2,192,384]{2,1,0:T(8,128)} %param.23) | copy-start | bytes 1769476
  401.1 147.6 %copy-start.31 = (f32[6,8,384]{2,1,0:T(8,128)}, f32[6,8,384]{2,1,0:T(8,128)S(1)}, u32[]{:S(2)}) copy-start(f32[6,8,384]{2,1,0:T(8,128)S(1)} %get-tuple-element.65) | copy-start | bytes 221188
  401.1 145.9 %copy-start.32 = (f32[6,8,384]{2,1,0:T(8,128)S(1)}, f32[6,8,384]{2,1,0:T(8,128)}, u32[]{:S(2)}) copy-start(f32[6,8,384]{2,1,0:T(8,128)} %reduce-scatter.31.cloned.1.call-done) | copy-start | bytes 221188
  473.5 77.1 %copy-start.14 = (f32[192,384]{1,0:T(8,128)}, f32[192,384]{1,0:T(8,128)S(1)}, u32[]{:S(2)}) copy-start(f32[192,384]{1,0:T(8,128)S(1)} %get-tuple-element.63) | copy-start | bytes 884740
  474.4 98.1 %copy-start.36 = (f32[384]{0:T(512)S(1)}, f32[384]{0:T(512)}, u32[]{:S(2)}) copy-start(f32[384]{0:T(512)} %copy-done.35) | copy-start | bytes 4612
  474.5 98.1 %copy-start.38 = (f32[512,1]{0,1:T(1,128)S(1)}, f32[512,1]{0,1:T(1,128)}, u32[]{:S(2)}) copy-start(f32[512,1]{0,1:T(1,128)} %copy-done.37) | copy-start | bytes 6148
  544.9 5.7 copy-start.17
  546.1 28.0 %copy-start.15 = (f32[192,384]{1,0:T(8,128)}, f32[192,384]{1,0:T(8,128)S(1)}, u32[]{:S(2)}) copy-start(f32[192,384]{1,0:T(8,128)S(1)} %get-tuple-element.61) | copy-start | bytes 884740
  546.1 72.6 %copy-start.34 = (f32[2,4,384]{2,1,0:T(4,128)S(1)}, f32[2,4,384]{2,1,0:T(4,128)}, u32[]{:S(2)}) copy-start(f32[2,4,384]{2,1,0:T(4,128)} %param.19) | copy-start | bytes 36868
  546.1 73.3 %copy-start.39 = (f32[4,384]{1,0:T(4,128)S(1)}, f32[4,384]{1,0:T(4,128)}, u32[]{:S(2)}) copy-start(f32[4,384]{1,0:T(4,128)} %param.14) | copy-start | bytes 18436
  547.0 73.0 %copy-start.3 = (f32[512,384]{1,0:T(8,128)S(1)}, f32[512,384]{1,0:T(8,128)}, u32[]{:S(2)}) copy-start(f32[512,384]{1,0:T(8,128)} %get-tuple-element.71) | copy-start | bytes 2359300
  550.6 91.1 %copy-start.9 = (f32[2,3,6,8,384]{4,3,2,1,0:T(8,128)S(1)}, f32[2,3,6,8,384]{4,3,2,1,0:T(8,128)}, u32[]{:S(2)}) copy-start(f32[2,3,6,8,384]{4,3,2,1,0:T(8,128)} %param.20) | copy-start | bytes 1327108
  574.1 69.5 %copy-start.21 = (f32[3,6,8,384]{3,2,1,0:T(8,128)S(1)}, f32[3,6,8,384]{3,2,1,0:T(8,128)}, u32[]{:S(2)}) copy-start(f32[3,6,8,384]{3,2,1,0:T(8,128)} %param.15) | copy-start | bytes 663556
  618.7 26.6 %copy-start.40 = (f32[4,384]{1,0:T(4,128)}, f32[4,384]{1,0:T(4,128)S(1)}, u32[]{:S(2)}) copy-start(f32[4,384]{1,0:T(4,128)S(1)} %get-tuple-element.69) | copy-start | bytes 18436
  (19 other events, 65.4 us)
Sparse Core Ops, SparseCore 0:
  59.0 12.7 reduce-scatter.12
  107.6 30.1 reduce-scatter.14
  140.1 14.1 reduce-scatter.20
  165.2 14.1 reduce-scatter.16
  184.7 14.1 all-gather.11
  200.3 13.2 all-gather.7
  215.9 27.3 reduce-scatter.22
  245.5 26.1 reduce-scatter.18
  287.9 9.0 reduce-scatter.24
  334.2 12.2 all-gather.13
Sparse Core Ops, SparseCore 1:
  62.1 41.5 all-gather.9
  110.7 41.3 all-gather.5
  338.5 61.6 reduce-scatter.30
  403.7 68.7 reduce-scatter.32
  476.0 68.9 reduce-scatter.34
  547.2 25.3 reduce-scatter.26
  575.9 65.8 reduce-scatter.28
